TPU v7x, 32 devices: a whole 2x2x4 slice. The times are simulated.
32 devices in a mesh: row: 8 (over y, x, core), col: 4 (over z).
Axes of the slice: x: 2, y: 2, z: 4, core: 2. Of those that a mesh axis runs over, the one named last changes fastest.
Arguments:
- panel_u: bfloat16 [2, 8, 1024, 160], P(None, 'row', 'col'), may hold values from -6 to 6
- panel_v: bfloat16 [2, 8, 1024, 160], P(None, 'row', 'col'), may hold values from -0.0625 to 0.0625
- panel_rank: int32 [2, 8], P(None, 'row'), may hold values from 32 to 160, as said below
- diag_inverse: bfloat16 [1024, 1024], P('col'), as said below
- tile_u: bfloat16 [2, 8, 4, 1024, 160], P(None, 'row', 'col'), may hold values from -6 to 6
- tile_v: bfloat16 [2, 8, 4, 1024, 160], P(None, 'row', 'col'), may hold values from -0.5 to 0.5
- tile_rank: int32 [2, 8, 4], P(None, 'row', 'col'), may hold values from 32 to 160, as said below
- sketch: bfloat16 [2, 8, 4, 1024, 160], P(None, 'row', 'col'), may hold values from -6 to 6
Outputs:
- new_u: float32 [2, 8, 4, 1024, 160], P(None, 'row', 'col')
- new_v: float32 [2, 8, 4, 1024, 160], P(None, 'row', 'col')
Inputs may be any that keep to these rules, and one draw needn't show every extreme that they name: `panel_rank`: some panel tile has rank 160. `tile_rank`: some trailing tile has rank 160. `diag_inverse`: lower triangular with diagonal entries of 1 to 2.
All inputs are finite; a program needn't handle non-finite values.
Results may differ from a plain program's by a relative error of at most 0.0037.
Values may be sent and summed in bfloat16 or wider, within the bound.
No kernel may reach another device: no remote copies, remote signals or barrier semaphores. Data moves between devices by JAX's collectives and lax.ppermute only.
A program may use at most 64 MiB of HBM per device.

v0:
```python
import math
import jax
import jax.numpy as jnp
from jax import lax
from jax.sharding import PartitionSpec as P


def spread(value, axis, source):
    kept = jnp.where(lax.axis_index(axis) == source, value, 0).astype(value.dtype)
    return lax.psum(kept, axis)


def recompress(old_u, old_v, row_u, row_s, col_u, col_s, omega, rank):
    high = lax.Precision.HIGHEST
    width = old_u.shape[1]
    keep_flag = jnp.arange(width, dtype=jnp.int32) < rank
    keep = keep_flag.astype(jnp.float32)
    keep_half = keep_flag.astype(jnp.bfloat16)
    ou_half = old_u * keep_half
    ov_half = old_v * keep_half
    om_half = omega * keep_half
    coupling = jnp.dot(row_s.T, col_s, preferred_element_type=jnp.float32)
    small_left = jnp.dot(ov_half.T, om_half, preferred_element_type=jnp.float32)
    small_right = jnp.dot(col_u.T, om_half, preferred_element_type=jnp.float32)
    ou = ou_half.astype(jnp.float32)
    ov = ov_half.astype(jnp.float32)
    ru = row_u.astype(jnp.float32)
    cu = col_u.astype(jnp.float32)
    sketched = jnp.dot(ou, small_left, precision=high)
    sketched = sketched - jnp.dot(
        ru, jnp.dot(coupling, small_right, precision=high), precision=high
    )
    gram = jnp.dot(sketched.T, sketched, precision=high) + jnp.diag(1.0 - keep)
    lower = jnp.linalg.cholesky(gram)
    basis = lax.linalg.triangular_solve(
        lower, sketched, left_side=False, lower=True, transpose_a=True
    )
    factor = math.sqrt(old_u.shape[0])
    right = jnp.dot(ov, jnp.dot(ou.T, basis, precision=high), precision=high)
    right = right - jnp.dot(
        cu,
        jnp.dot(coupling.T, jnp.dot(ru.T, basis, precision=high), precision=high),
        precision=high,
    )
    return (basis * factor, right / factor)


def on_device(panel_u, panel_v, panel_rank, diag_inverse, tile_u, tile_v, tile_rank, sketch):
    width = panel_u.shape[3]
    keep = (
        jnp.arange(width, dtype=jnp.int32)[None, None, None, :] < panel_rank[:, :, None, None]
    ).astype(jnp.bfloat16)
    full_u, full_v = (
        lax.all_gather(panel_u * keep, "col", axis=2, tiled=True),
        lax.all_gather(panel_v * keep, "col", axis=2, tiled=True),
    )
    inverse = lax.all_gather(diag_inverse, "col", axis=0, tiled=True)
    solved = jnp.einsum(
        "ab,tsbr->tsar", inverse, full_v, preferred_element_type=jnp.float32
    ).astype(jnp.bfloat16)
    col_count = lax.axis_size("col")
    col_place = lax.axis_index("col")
    results_u = []
    results_v = []
    for column in range(tile_u.shape[0]):
        source = column * col_count + col_place
        col_u, col_s = (spread(full_u[0, 0], "row", source), spread(solved[0, 0], "row", source))
        fresh_u, fresh_v = recompress(
            tile_u[column, 0, 0],
            tile_v[column, 0, 0],
            full_u[1, 0],
            solved[1, 0],
            col_u,
            col_s,
            sketch[column, 0, 0],
            tile_rank[column, 0, 0],
        )
        results_u.append(fresh_u)
        results_v.append(fresh_v)
    stacked_u = jnp.stack(results_u)[:, None, None]
    stacked_v = jnp.stack(results_v)[:, None, None]
    return (stacked_u, stacked_v)


def solution(mesh):
    placed = (
        P(None, "row", "col", None),
        P(None, "row", "col", None),
        P(None, "row"),
        P("col", None),
        P(None, "row", "col", None, None),
        P(None, "row", "col", None, None),
        P(None, "row", "col"),
        P(None, "row", "col", None, None),
    )
    return jax.shard_map(
        on_device,
        mesh=mesh,
        in_specs=placed,
        out_specs=(P(None, "row", "col", None, None), P(None, "row", "col", None, None)),
        check_vma=False,
    )
```

profile of v0, /device:TPU:0, one launch (start us, length us, event | category | flops | bytes accessed | tf_op | source)
XLA Modules:
  0.0 269.2 jit_solution(11368111475773620207)
XLA Ops:
  7.2 0.7 all-gather.2.cloned.1.call-update
  8.0 1.3 fusion.77
  9.3 0.6 fusion.71
  10.6 0.7 convert_subtract_fusion
  11.3 0.7 compare_convert_fusion
  12.0 1.1 bitcast_multiply_fusion.15
  13.1 1.4 fusion.24
  14.9 27.4 %all_gather.9 = bf16[2,1,1024,160]{2,3,0,1:T(8,128)(2,1)S(1)} all-gather(bf16[2,1,256,160]{2,3,0,1:T(8,128)(2,1)S(1)} %get-tuple-element.50), channel_id=1, replica_groups=mesh['row'=8,'col'=4] {'col'}, dimensions={2}, use_global_device_ids=true | all-gather | bytes 819200 | tf_op jit(solution)/shard_map/all_gather | solution.py:54
  42.3 26.6 %all_gather.10 = bf16[2,1,1024,160]{2,3,0,1:T(8,128)(2,1)S(1)} all-gather(bf16[2,1,256,160]{2,3,0,1:T(8,128)(2,1)S(1)} %get-tuple-element.51), channel_id=1, replica_groups=mesh['row'=8,'col'=4] {'col'}, dimensions={2}, use_global_device_ids=true | all-gather | bytes 819200 | tf_op jit(solution)/shard_map/all_gather | solution.py:55
  68.9 0.9 select_bitcast_fusion.2
  69.8 6.8 %all-gather.2.cloned.1.call-done = bf16[1024,1024]{1,0:T(8,128)(2,1)} async-done(((bf16[256,1024]{1,0:T(8,128)(2,1)}), bf16[1024,1024]{1,0:T(8,128)(2,1)}) %all-gather.2.cloned.1.call-update) | async-done | bytes 2097168 | tf_op jit(solution)/shard_map/all_gather | solution.py:57
  76.6 2.5 fusion.5
  79.1 0.9 select_bitcast_fusion.3
  81.2 1.5 fusion.45
  82.7 55.3 %all-reduce.6.cloned.1.call-done = (bf16[1024,160]{0,1:T(8,128)(2,1)}, bf16[1024,160]{0,1:T(8,128)(2,1)}, bf16[1024,160]{0,1:T(8,128)(2,1)}, bf16[1024,160]{0,1:T(8,128)(2,1)}) async-done(((bf16[1024,160]{0,1:T(8,128)(2,1)}, bf16[1024,160]{0,1:T(8,128)(2,1)}, bf16[1024,160]{0,1:T(8,128)(2,1)}, bf16[1024,160]{0,1:T(8,128)(2,1)}), (bf16[1024,160]{0,1:T(8,128)(2,1)}, bf16[1024,160]{0,1:T(8,128)(2,1)}, ...) | async-done | bytes 1310736 | tf_op jit(solution)/shard_map/psum | solution.py:10
  138.0 1.4 fusion.23
  139.4 1.2 fusion.35
  141.4 0.7 convolution_add_fusion
  142.3 11.7 %cholesky.174 = f32[128,128]{1,0:T(8,128)S(1)} custom-call(f32[128,128]{1,0:T(8,128)S(1)} %cholesky.211), custom_call_target="Cholesky" | custom-call | tf_op jit(solution)/shard_map/jit(cholesky)/cholesky | solution.py:34
  154.0 0.7 select_reduce_fusion
  154.7 1.4 fusion.27
  156.1 1.2 fusion.36
  158.1 0.7 convolution_add_fusion.1
  159.0 11.9 %cholesky.136 = f32[128,128]{1,0:T(8,128)S(1)} custom-call(f32[128,128]{1,0:T(8,128)S(1)} %cholesky.208), custom_call_target="Cholesky" | custom-call | tf_op jit(solution)/shard_map/jit(cholesky)/cholesky | solution.py:34
  170.9 10.6 %custom-call.15 = f32[1,128,128]{1,2,0:T(8,128)S(1)} custom-call(f32[1,128,128]{2,1,0:T(8,128)} %get-tuple-element.45), custom_call_target="InvertDiagBlocksLowerTriangular" | custom-call | tf_op jit(solution)/shard_map/jit(cholesky)/cholesky | solution.py:34
  181.9 2.9 %cholesky.194 = f32[32,32]{1,0:T(8,128)S(1)} custom-call(f32[32,32]{1,0:T(8,128)S(1)} %convolution_subtract_fusion.6), custom_call_target="Cholesky" | custom-call | tf_op jit(solution)/shard_map/jit(cholesky)/cholesky | solution.py:34
  184.8 0.6 compare_reduce_fusion
  185.5 0.6 compare_reduce_fusion.1
  187.4 0.6 copy-done.6
  188.1 9.8 %custom-call.13 = f32[1,128,128]{1,2,0:T(8,128)S(1)} custom-call(f32[1,128,128]{2,1,0:T(8,128)S(1)} %get-tuple-element.43), custom_call_target="InvertDiagBlocksLowerTriangular" | custom-call | tf_op jit(solution)/shard_map/jit(cholesky)/cholesky | solution.py:34
  198.2 2.9 %cholesky.156 = f32[32,32]{1,0:T(8,128)S(1)} custom-call(f32[32,32]{1,0:T(8,128)S(1)} %convolution_subtract_fusion.7), custom_call_target="Cholesky" | custom-call | tf_op jit(solution)/shard_map/jit(cholesky)/cholesky | solution.py:34
  201.8 0.6 compare_reduce_fusion.3
  203.6 0.7 select_select_fusion.1
  204.3 0.7 slice.139
  205.0 0.8 slice_bitcast_fusion.13
  206.0 0.7 pad_maximum_fusion.6
  206.6 19.7 %custom-call.14 = f32[2,128,128]{1,2,0:T(8,128)S(1)} custom-call(f32[2,128,128]{2,1,0:T(8,128)S(1)} %get-tuple-element.58), custom_call_target="InvertDiagBlocksLowerTriangular" | custom-call | tf_op jit(solution)/shard_map/triangular_solve/custom-call.0 | solution.py:35
  226.3 0.6 copy-done.10
  227.6 1.2 convolution_subtract_fusion.5
  228.8 1.0 fusion.68
  230.3 1.2 fusion.20
  231.5 20.5 %custom-call.16 = f32[2,128,128]{1,2,0:T(8,128)S(1)} custom-call(f32[2,128,128]{2,1,0:T(8,128)} %get-tuple-element.59), custom_call_target="InvertDiagBlocksLowerTriangular" | custom-call | tf_op jit(solution)/shard_map/triangular_solve/custom-call.0 | solution.py:35
  252.0 0.6 copy-done.11
  252.6 0.6 fusion.13
  253.3 1.1 convolution_subtract_fusion.4
  254.4 1.0 fusion.65
  260.1 1.1 maximum_bitcast_fusion.1
  261.2 1.2 maximum_bitcast_fusion
  (68 shorter events, 11.1 us)
Async XLA Ops:
  7.2 7.3 %copy-start.12 = (bf16[2,1,1,1024,160]{3,4,2,1,0:T(8,128)(2,1)S(1)}, bf16[2,1,1,1024,160]{3,4,2,1,0:T(8,128)(2,1)}, u32[]{:S(2)}) copy-start(bf16[2,1,1,1024,160]{3,4,2,1,0:T(8,128)(2,1)} %param.18) | copy-start | bytes 1966084
  7.2 7.3 %copy-start.4 = (bf16[2,1,1,1024,160]{3,4,2,1,0:T(8,128)(2,1)S(1)}, bf16[2,1,1,1024,160]{3,4,2,1,0:T(8,128)(2,1)}, u32[]{:S(2)}) copy-start(bf16[2,1,1,1024,160]{3,4,2,1,0:T(8,128)(2,1)} %param.16) | copy-start | bytes 1966084
  7.2 69.5 %all-gather.2.cloned.1.call-start = ((), (), s32[]{:S(2)}) async-start(), calls=%async_computation | async-start | bytes 2621440 | tf_op jit(solution)/shard_map/all_gather | solution.py:57
  7.9 130.1 %all-reduce.6.cloned.1.call-start = ((), (), s32[]{:S(2)}) async-start(), calls=%async_computation.1 | async-start | bytes 2621440 | tf_op jit(solution)/shard_map/psum | solution.py:10
  79.1 60.3 %copy-start = (bf16[2,1,1024,160]{2,3,0,1:T(8,128)(2,1)}, bf16[2,1,1024,160]{2,3,0,1:T(8,128)(2,1)S(1)}, u32[]{:S(2)}) copy-start(bf16[2,1,1024,160]{2,3,0,1:T(8,128)(2,1)S(1)} %fusion.5) | copy-start | bytes 1966084
  79.1 1.6 copy-start.2
  142.1 14.0 %copy-start.1 = (bf16[2,1,1024,160]{2,3,0,1:T(8,128)(2,1)S(1)}, bf16[2,1,1024,160]{2,3,0,1:T(8,128)(2,1)}, u32[]{:S(2)}) copy-start(bf16[2,1,1024,160]{2,3,0,1:T(8,128)(2,1)} %copy-done) | copy-start | bytes 1966084
  187.4 0.7 copy-start.6
  226.3 0.7 copy-start.10
  227.6 2.7 %copy-start.3 = (bf16[2,1,1,1024,160]{3,4,2,1,0:T(8,128)(2,1)S(1)}, bf16[2,1,1,1024,160]{3,4,2,1,0:T(8,128)(2,1)}, u32[]{:S(2)}) copy-start(bf16[2,1,1,1024,160]{3,4,2,1,0:T(8,128)(2,1)} %param.15) | copy-start | bytes 1966084
  252.0 0.7 copy-start.11
  256.4 1.1 copy-start.5
  256.4 1.1 copy-start.9
  257.5 1.6 copy-start.8
  258.6 1.0 copy-start.7
Sparse Core Ops, SparseCore 0:
  9.6 67.0 all-gather.1
  80.6 57.3 all-reduce.5
where the time goes:
time: 270 us; the launch traced here: 269 us
  other arithmetic  103 us (38%)
  waiting for transfers between devices  62.8 us (23%)
  blocking collectives  54 us (20%)
  matrix products  26.2 us (10%)
  between operations  17.2 us (6%)
  local copies, waits for them, and re-layouts  5.59 us (2%)
    psum x1, waiting for transfers between devices, spread(): return lax.psum(kept, axis)  55.3 us
    another operation x14, other arithmetic, recompress(): lower = jnp.linalg.cholesky(gram)  53.1 us
    another operation x8, other arithmetic, recompress(): lax.linalg.triangular_solve(lower, sketched, left_side=False, lower=True,...  41.6 us
    all_gather x1, blocking collectives, on_device(): lax.all_gather(panel_u * keep, 'col', axis=2, tiled=True)  27.4 us
    all_gather x1, blocking collectives, on_device(): lax.all_gather(panel_v * keep, 'col', axis=2, tiled=True)  26.6 us
    all_gather x1, waiting for transfers between devices, on_device(): inverse = lax.all_gather(diag_inverse, 'col', axis=0, tiled=True)  6.83 us
    another operation x6, matrix products, recompress(): lax.linalg.triangular_solve(lower, sketched, left_side=False, lower=True,...  5.61 us
  transfers between devices with their start and end apart: 2, of which 2 were waited for; matrix products, arithmetic and copies ran while one was open for 4% of the time, Pallas kernels for 0%

commit v1 on v0

--- a/solution.py
+++ b/solution.py
@@ -7,7 +7,7 @@
 
 def spread(value, axis, source):
     kept = jnp.where(lax.axis_index(axis) == source, value, 0).astype(value.dtype)
-    return lax.psum(kept, axis)
+    return jnp.sum(lax.all_gather(kept, axis), axis=0)
 
 
 def recompress(old_u, old_v, row_u, row_s, col_u, col_s, omega, rank):

time: 270 us -> 294 us (1.089)
  waiting for transfers between devices: 62.8 us -> 90.5 us
  other arithmetic: 103 us -> 110 us
  blocking collectives: 54 us -> 49.4 us
  matrix products: 26.2 us -> 23 us
    all_gather x0 -> x4, waiting for transfers between devices: none -> 77.8 us  [spread(): return jnp.sum(lax.all_gather(kept, axis), axis=0)]
    psum x1 -> x0, waiting for transfers between devices: 55.3 us -> none  [spread(): return lax.psum(kept, axis)]
    reduce_sum x0 -> x4, other arithmetic: none -> 8.91 us  [spread(): return jnp.sum(lax.all_gather(kept, axis), axis=0)]
    all_gather x1, waiting for transfers between devices: 6.83 us -> 11.3 us  [on_device(): inverse = lax.all_gather(diag_inverse, 'col', axis=0, tiled=True)]
    all_gather x1, blocking collectives: 27.4 us -> 23.8 us  [on_device(): lax.all_gather(panel_u * keep, 'col', axis=2, tiled=True)]
  transfers between devices with their start and end apart: 2 -> 5, of which waited for: 2 -> 5; matrix products, arithmetic and copies ran while one was open for 4% -> 18% of each run, Pallas kernels for 0% -> 0%
where the time goes in v1:
time: 294 us; the launch traced here: 293 us
  other arithmetic  110 us (37%)
  waiting for transfers between devices  90.5 us (31%)
  blocking collectives  49.4 us (17%)
  matrix products  23 us (8%)
  between operations  17 us (6%)
  local copies, waits for them, and re-layouts  2.95 us (1%)
    all_gather x4, waiting for transfers between devices, spread(): return jnp.sum(lax.all_gather(kept, axis), axis=0)  77.8 us
    another operation x14, other arithmetic, recompress(): lower = jnp.linalg.cholesky(gram)  51.6 us
    another operation x8, other arithmetic, recompress(): lax.linalg.triangular_solve(lower, sketched, left_side=False, lower=True,...  41 us
    all_gather x1, blocking collectives, on_device(): lax.all_gather(panel_v * keep, 'col', axis=2, tiled=True)  25.7 us
    all_gather x1, blocking collectives, on_device(): lax.all_gather(panel_u * keep, 'col', axis=2, tiled=True)  23.8 us
    all_gather x1, waiting for transfers between devices, on_device(): inverse = lax.all_gather(diag_inverse, 'col', axis=0, tiled=True)  11.3 us
    reduce_sum x4, other arithmetic, spread(): return jnp.sum(lax.all_gather(kept, axis), axis=0)  8.91 us
  transfers between devices with their start and end apart: 5, of which 5 were waited for; matrix products, arithmetic and copies ran while one was open for 18% of the time, Pallas kernels for 0%

profile of v1, /device:TPU:0, one launch (start us, length us, event | category | flops | bytes accessed | tf_op | source)
XLA Modules:
  0.0 293.3 jit_solution(6367466076463747102)
XLA Ops:
  7.2 0.7 all-gather.10.cloned.1.call-update
  8.0 0.7 compare_convert_fusion
  8.7 1.1 bitcast_multiply_fusion.15
  9.8 23.8 %all_gather.25 = bf16[2,1,1024,160]{2,3,0,1:T(8,128)(2,1)S(1)} all-gather(bf16[2,1,256,160]{2,3,0,1:T(8,128)(2,1)S(1)} %get-tuple-element.48), channel_id=1, replica_groups=mesh['row'=8,'col'=4] {'col'}, dimensions={2}, use_global_device_ids=true | all-gather | bytes 819200 | tf_op jit(solution)/shard_map/all_gather | solution.py:54
  33.6 0.9 select_bitcast_fusion.2
  34.5 0.7 all-gather.18.cloned.1.call-update
  35.3 25.7 %all_gather.26 = bf16[2,1,1024,160]{2,3,0,1:T(8,128)(2,1)S(1)} all-gather(bf16[2,1,256,160]{2,3,0,1:T(8,128)(2,1)S(1)} %get-tuple-element.49), channel_id=1, replica_groups=mesh['row'=8,'col'=4] {'col'}, dimensions={2}, use_global_device_ids=true | all-gather | bytes 819200 | tf_op jit(solution)/shard_map/all_gather | solution.py:55
  60.9 11.3 %all-gather.10.cloned.1.call-done = bf16[1024,1024]{1,0:T(8,128)(2,1)} async-done(((bf16[256,1024]{1,0:T(8,128)(2,1)}), bf16[1024,1024]{1,0:T(8,128)(2,1)}) %all-gather.10.cloned.1.call-update) | async-done | bytes 2097168 | tf_op jit(solution)/shard_map/all_gather | solution.py:57
  72.2 2.5 fusion.5
  74.7 0.9 select_bitcast_fusion.3
  75.7 0.7 fusion.77
  76.3 0.6 fusion.72
  77.0 0.7 fusion.71
  77.6 0.7 convert_subtract_fusion
  78.4 1.3 fusion.24
  79.7 2.0 fusion.28
  81.7 0.6 convert_subtract_fusion.1
  82.4 1.4 fusion.45
  84.3 19.7 %all-gather.14.cloned.1.call-done = bf16[8,1,1024,160]{2,3,1,0:T(8,128)(2,1)} async-done(((bf16[1,1,1024,160]{2,3,1,0:T(8,128)(2,1)}), bf16[8,1,1024,160]{2,3,1,0:T(8,128)(2,1)}) %all-gather.14.cloned.1.call-update) | async-done | bytes 2621456 | tf_op jit(solution)/shard_map/all_gather | solution.py:10
  104.0 2.2 bitcast_reduce_fusion.2
  106.2 29.7 %all-gather.18.cloned.1.call-done = bf16[8,1,1024,160]{2,3,1,0:T(8,128)(2,1)} async-done(((bf16[1,1,1024,160]{2,3,1,0:T(8,128)(2,1)}), bf16[8,1,1024,160]{2,3,1,0:T(8,128)(2,1)}) %all-gather.18.cloned.1.call-update) | async-done | bytes 2621456 | tf_op jit(solution)/shard_map/all_gather | solution.py:10
  135.9 2.3 bitcast_reduce_fusion
  138.2 1.0 fusion.23
  139.2 1.0 fusion.27
  140.2 28.0 %all-gather.16.cloned.1.call-done = bf16[8,1,1024,160]{2,3,1,0:T(8,128)(2,1)} async-done(((bf16[1,1,1024,160]{2,3,1,0:T(8,128)(2,1)}), bf16[8,1,1024,160]{2,3,1,0:T(8,128)(2,1)}) %all-gather.16.cloned.1.call-update) | async-done | bytes 2621456 | tf_op jit(solution)/shard_map/all_gather | solution.py:10
  168.2 2.2 bitcast_reduce_fusion.1
  171.5 0.7 convolution_add_fusion
  172.4 11.7 %cholesky.174 = f32[128,128]{1,0:T(8,128)S(1)} custom-call(f32[128,128]{1,0:T(8,128)S(1)} %cholesky.211), custom_call_target="Cholesky" | custom-call | tf_op jit(solution)/shard_map/jit(cholesky)/cholesky | solution.py:34
  184.2 9.8 %custom-call.15 = f32[1,128,128]{1,2,0:T(8,128)S(1)} custom-call(f32[1,128,128]{2,1,0:T(8,128)S(1)} %get-tuple-element.43), custom_call_target="InvertDiagBlocksLowerTriangular" | custom-call | tf_op jit(solution)/shard_map/jit(cholesky)/cholesky | solution.py:34
  194.3 2.9 cholesky.194
  197.2 0.6 compare_reduce_fusion.1
  199.8 0.6 slice_bitcast_fusion.10
  200.9 2.2 bitcast_reduce_fusion.3
  203.4 0.7 copy-done
  205.0 0.7 convolution_add_fusion.1
  205.9 11.7 %cholesky.136 = f32[128,128]{1,0:T(8,128)S(1)} custom-call(f32[128,128]{1,0:T(8,128)S(1)} %cholesky.208), custom_call_target="Cholesky" | custom-call | tf_op jit(solution)/shard_map/jit(cholesky)/cholesky | solution.py:34
  217.6 0.7 compare_reduce_fusion.3
  218.3 9.8 %custom-call.13 = f32[1,128,128]{1,2,0:T(8,128)S(1)} custom-call(f32[1,128,128]{2,1,0:T(8,128)S(1)} %get-tuple-element.41), custom_call_target="InvertDiagBlocksLowerTriangular" | custom-call | tf_op jit(solution)/shard_map/jit(cholesky)/cholesky | solution.py:34
  228.5 2.9 cholesky.156
  231.4 0.7 compare_reduce_fusion.2
  233.5 0.7 pad_maximum_fusion.6
  234.2 19.7 %custom-call.16 = f32[2,128,128]{1,2,0:T(8,128)S(1)} custom-call(f32[2,128,128]{2,1,0:T(8,128)S(1)} %get-tuple-element.57), custom_call_target="InvertDiagBlocksLowerTriangular" | custom-call | tf_op jit(solution)/shard_map/triangular_solve/custom-call.0 | solution.py:35
  254.5 1.1 convolution_subtract_fusion.4
  257.0 20.5 %custom-call.14 = f32[2,128,128]{1,2,0:T(8,128)S(1)} custom-call(f32[2,128,128]{2,1,0:T(8,128)} %get-tuple-element.56), custom_call_target="InvertDiagBlocksLowerTriangular" | custom-call | tf_op jit(solution)/shard_map/triangular_solve/custom-call.0 | solution.py:35
  277.5 0.6 copy-done.14
  279.2 1.0 fusion.68
  283.9 1.2 maximum_bitcast_fusion
  285.6 1.2 maximum_bitcast_fusion.1
  (89 shorter events, 12.3 us)
Async XLA Ops:
  7.2 65.1 %all-gather.10.cloned.1.call-start = ((), (), s32[]{:S(2)}) async-start(), calls=%async_computation | async-start | bytes 2621440 | tf_op jit(solution)/shard_map/all_gather | solution.py:57
  7.9 96.1 %all-gather.14.cloned.1.call-start = ((), (), s32[]{:S(2)}) async-start(), calls=%async_computation.2 | async-start | bytes 2949120 | tf_op jit(solution)/shard_map/all_gather | solution.py:10
  34.5 101.4 %all-gather.18.cloned.1.call-start = ((), (), s32[]{:S(2)}) async-start(), calls=%async_computation.4 | async-start | bytes 2949120 | tf_op jit(solution)/shard_map/all_gather | solution.py:10
  35.2 133.0 %all-gather.16.cloned.1.call-start = ((), (), s32[]{:S(2)}) async-start(), calls=%async_computation.3 | async-start | bytes 2949120 | tf_op jit(solution)/shard_map/all_gather | solution.py:10
  60.9 14.7 %copy-start.15 = (s32[2,1,1]{0,2,1:T(1,128)S(1)}, s32[2,1,1]{0,2,1:T(1,128)}, u32[]{:S(2)}) copy-start(s32[2,1,1]{0,2,1:T(1,128)} %param.17) | copy-start | bytes 28
  60.9 17.4 %copy-start.8 = (bf16[2,1,1,1024,160]{3,4,2,1,0:T(8,128)(2,1)S(1)}, bf16[2,1,1,1024,160]{3,4,2,1,0:T(8,128)(2,1)}, u32[]{:S(2)}) copy-start(bf16[2,1,1,1024,160]{3,4,2,1,0:T(8,128)(2,1)} %param.16) | copy-start | bytes 1966084
  74.7 7.7 %copy-start.6 = (bf16[2,1,1,1024,160]{3,4,2,1,0:T(8,128)(2,1)S(1)}, bf16[2,1,1,1024,160]{3,4,2,1,0:T(8,128)(2,1)}, u32[]{:S(2)}) copy-start(bf16[2,1,1,1024,160]{3,4,2,1,0:T(8,128)(2,1)} %param.15) | copy-start | bytes 1966084
  75.6 125.3 %all-gather.12.cloned.1.call-start = ((), (), s32[]{:S(2)}) async-start(), calls=%async_computation.1 | async-start | bytes 2949120 | tf_op jit(solution)/shard_map/all_gather | solution.py:10
  106.2 34.0 %copy-start.2 = (bf16[1024,160]{0,1:T(8,128)(2,1)}, bf16[1024,160]{0,1:T(8,128)(2,1)S(1)}, u32[]{:S(2)}) copy-start(bf16[1024,160]{0,1:T(8,128)(2,1)S(1)} %bitcast_reduce_fusion.2) | copy-start | bytes 983044
  135.9 2.3 copy-start.16
  138.2 32.3 %copy-start.4 = (bf16[1024,160]{0,1:T(8,128)(2,1)}, bf16[1024,160]{0,1:T(8,128)(2,1)S(1)}, u32[]{:S(2)}) copy-start(bf16[1024,160]{0,1:T(8,128)(2,1)S(1)} %bitcast_reduce_fusion) | copy-start | bytes 983044
  168.2 2.5 copy-start.13
  199.8 4.3 %copy-start.12 = (f32[160,160]{1,0:T(8,128)S(1)}, f32[160,160]{1,0:T(8,128)}, u32[]{:S(2)}) copy-start(f32[160,160]{1,0:T(8,128)} %fusion.27) | copy-start | bytes 307204
  199.8 0.7 copy-start.10
  203.4 0.7 copy-start
  205.0 28.5 %copy-start.11 = (f32[1,128,128]{2,1,0:T(8,128)S(1)}, f32[1,128,128]{2,1,0:T(8,128)}, u32[]{:S(2)}) copy-start(f32[1,128,128]{2,1,0:T(8,128)} %slice_bitcast_fusion.10) | copy-start | bytes 196612
  205.8 50.1 %copy-start.7 = (bf16[2,1,1,1024,160]{3,4,2,1,0:T(8,128)(2,1)S(1)}, bf16[2,1,1,1024,160]{3,4,2,1,0:T(8,128)(2,1)}, u32[]{:S(2)}) copy-start(bf16[2,1,1,1024,160]{3,4,2,1,0:T(8,128)(2,1)} %param.15) | copy-start | bytes 1966084
  277.5 0.7 copy-start.14
  280.2 1.6 copy-start.9
  280.7 1.6 copy-start.1
  281.3 2.2 copy-start.5
  283.4 1.7 copy-start.3
Sparse Core Ops, SparseCore 0:
  9.5 62.6 all-gather.9
  74.1 29.8 all-gather.13
  105.9 29.9 all-gather.17
  138.2 29.9 all-gather.15
  170.5 30.3 all-gather.11
